TPU v7x, 128 devices: a whole 4x4x4 slice. The times are simulated.
128 devices in a mesh: dp: 32 (over z, x, core), head: 4 (over y).
Axes of the slice: x: 4, y: 4, z: 4, core: 2. Of those that a mesh axis runs over, the one named last changes fastest.
Arguments:
- hidden: bfloat16 [1024, 2048], P('dp'), may hold values from -6 to 6
- attn_gain: float32 [2048], replicated, may hold values from 0.1 to 1.9
- w_query: bfloat16 [2048, 3072], P(None, 'head'), may hold values from -0.125 to 0.125
- w_latent: bfloat16 [2048, 576], P(None, 'head'), may hold values from -0.125 to 0.125
- latent_gain: float32 [512], replicated, may hold values from 0.1 to 1.9
- w_key_up: bfloat16 [16, 128, 512], P('head'), may hold values from -0.5 to 0.5
- w_value_up: bfloat16 [16, 512, 128], P('head'), may hold values from -0.25 to 0.25
- w_out: bfloat16 [2048, 2048], P('head'), may hold values from -0.125 to 0.125
- kv_cache: bfloat16 [1024, 128, 576], P('dp'), may hold values from -110 to 110
- lengths: int32 [1024], P('dp'), may hold values from 1 to 128, 65536 in all
- live_mask: int32 [1024], P('dp'), may hold values 0 or 1
- mlp_gain: float32 [2048], replicated, may hold values from 0.1 to 1.9
- w_router: bfloat16 [2048, 64], replicated, may hold values from -0.125 to 0.125
- routes: int32 [1024, 6], P('dp'), may hold values from 0 to 63, all different within a row; in each aligned block of 32 rows (0 to 31, 32 to 63, ...) at most 6 rows name the same one
- w_experts_in: bfloat16 [64, 2048, 2, 1408], P('dp', None, None, 'head'), may hold values from -0.125 to 0.125
- w_experts_out: bfloat16 [64, 1408, 2048], P('dp', 'head'), may hold values from -0.15625 to 0.15625
- w_shared_in: bfloat16 [2048, 2, 1408], P(None, None, 'head'), may hold values from -0.125 to 0.125
- w_shared_out: bfloat16 [1408, 2048], P('head'), may hold values from -0.15625 to 0.15625
Outputs:
- output: bfloat16 [1024, 2048], P('dp', 'head')
Inputs may be any that keep to these rules, and one draw needn't show every extreme that they name: Among the routes of one device's 32 rows no expert is named more than 6 times, a bound that some block reaches. Request t has cached positions 0 to lengths[t] - 1; some request has 128.
All inputs are finite; a program needn't handle non-finite values. No bound on the sum of `lengths` or of `live_mask` on one device may be relied on, other than what follows from the above.
Results may differ from a plain program's by a relative error of at most 0.02.
The roundings to bfloat16 on the way count: a program that leaves them out, or rounds other values in their place, can miss the bound.
Values may be sent and summed in bfloat16 or wider, within the bound.
A program may use at most 128 MiB of HBM per device.

v0:
```python
import math
import jax
import jax.numpy as jnp
from jax import lax
from jax.sharding import PartitionSpec as P

NOPE = 128
ROPE = 64
VDIM = 128
LAT = 512
norm_eps = 1e-06
rope_theta = 50000.0
route_scale = 2.446


def rms_norm(values, weights):
    mean_square = jnp.mean(values * values, axis=-1, keepdims=True)
    return values * lax.rsqrt(mean_square + norm_eps) * weights


def rotary(values, positions):
    half_size = values.shape[-1] // 2
    frequency = rope_theta ** (-jnp.arange(half_size, dtype=jnp.float32) / half_size)
    angles = positions.reshape((-1,) + (1,) * (values.ndim - 1)) * frequency
    first_half = values[..., :half_size]
    second_half = values[..., half_size:]
    cosine = jnp.cos(angles)
    sine_part = jnp.sin(angles)
    return jnp.concatenate(
        [
            first_half * cosine - second_half * sine_part,
            second_half * cosine + first_half * sine_part,
        ],
        axis=-1,
    )


def body(
    hidden,
    attn_gain,
    w_query,
    w_latent,
    latent_gain,
    w_key_up,
    w_value_up,
    w_out,
    kv_cache,
    lengths,
    live_mask,
    mlp_gain,
    w_router,
    routes,
    w_experts_in,
    w_experts_out,
    w_shared_in,
    w_shared_out,
):
    request_count = hidden.shape[0]
    model_width = hidden.shape[1]
    local_heads = w_key_up.shape[0]
    cache_length = kv_cache.shape[1]
    head_count = lax.axis_size("head")
    share_width = model_width // head_count
    column_start = lax.axis_index("head") * share_width
    dp_count = lax.axis_size("dp")
    local_experts = w_experts_in.shape[0]
    expert_total = local_experts * dp_count
    top_count = routes.shape[1]
    capacity = max(2, 2 * top_count * request_count // expert_total)
    normed = rms_norm(hidden.astype(jnp.float32), attn_gain).astype(jnp.bfloat16)
    query_all = jnp.dot(normed, w_query, preferred_element_type=jnp.float32).reshape(
        request_count, local_heads, NOPE + ROPE
    )
    positions = lengths.astype(jnp.float32)
    query_nope = query_all[..., :NOPE].astype(jnp.bfloat16)
    query_rope = rotary(query_all[..., NOPE:], positions).astype(jnp.bfloat16)
    query_latent = jnp.einsum(
        "rhn,hnc->rhc", query_nope, w_key_up, preferred_element_type=jnp.float32
    ).astype(jnp.bfloat16)
    fresh_part = jnp.dot(normed, w_latent, preferred_element_type=jnp.float32).astype(jnp.bfloat16)
    fresh_kv = lax.all_gather(fresh_part, "head", axis=1, tiled=True)
    latent_new = rms_norm(fresh_kv[:, :LAT].astype(jnp.float32), latent_gain)
    rope_new = rotary(fresh_kv[:, LAT:].astype(jnp.float32), positions)
    key_new = jnp.concatenate([latent_new, rope_new], axis=-1).astype(jnp.bfloat16)
    query_full = jnp.concatenate([query_latent, query_rope], axis=-1)
    inverse_root = 1.0 / math.sqrt(NOPE + ROPE)
    scores = (
        jnp.einsum("rhc,rjc->rhj", query_full, kv_cache, preferred_element_type=jnp.float32)
        * inverse_root
    )
    in_cache = jnp.arange(cache_length, dtype=jnp.int32)[None, :] < lengths[:, None]
    scores = jnp.where(in_cache[:, None, :], scores, -jnp.inf)
    score_new = (
        jnp.einsum("rhc,rc->rh", query_full, key_new, preferred_element_type=jnp.float32)
        * inverse_root
    )
    highest = jnp.maximum(jnp.max(scores, axis=-1), score_new)
    weights_cached = jnp.exp(scores - highest[..., None])
    weight_new = jnp.exp(score_new - highest)
    denominator = jnp.sum(weights_cached, axis=-1) + weight_new
    probabilities = (weights_cached / denominator[..., None]).astype(jnp.bfloat16)
    prob_new = (weight_new / denominator).astype(jnp.bfloat16)
    context = jnp.einsum(
        "rhj,rjc->rhc", probabilities, kv_cache[..., :LAT], preferred_element_type=jnp.float32
    )
    context = (
        context
        + prob_new.astype(jnp.float32)[..., None] * key_new[:, None, :LAT].astype(jnp.float32)
    ).astype(jnp.bfloat16)
    values = jnp.einsum(
        "rhc,hcv->rhv", context, w_value_up, preferred_element_type=jnp.float32
    ).astype(jnp.bfloat16)
    partial_value = jnp.dot(
        values.reshape(request_count, local_heads * VDIM), w_out, preferred_element_type=jnp.float32
    )
    attention = lax.psum(partial_value.astype(jnp.bfloat16), "head").astype(jnp.float32)
    mixed_rows = (hidden.astype(jnp.float32) + attention).astype(jnp.bfloat16)
    ffn_input = rms_norm(mixed_rows.astype(jnp.float32), mlp_gain).astype(jnp.bfloat16)
    mixed_share = lax.dynamic_slice_in_dim(mixed_rows, column_start, share_width, 1)
    logits = jnp.dot(ffn_input, w_router, preferred_element_type=jnp.float32)
    chosen = jax.nn.sigmoid(jnp.take_along_axis(logits, routes, axis=1))
    route_weight = (
        route_scale
        * live_mask.astype(jnp.float32)[:, None]
        * chosen
        / jnp.sum(chosen, axis=1, keepdims=True)
    )
    pair_count = request_count * top_count
    flat_routes = routes.reshape(pair_count)
    live_pairs = jnp.repeat(live_mask, top_count)
    member = (
        (flat_routes[:, None] == jnp.arange(expert_total, dtype=jnp.int32)[None, :])
        & (live_pairs[:, None] == 1)
    ).astype(jnp.int32)
    earlier = jnp.cumsum(member, axis=0) - member
    slot_rank = jnp.sum(earlier * member, axis=1)
    slot_total = expert_total * capacity
    buffer_slot = jnp.where(live_pairs == 1, flat_routes * capacity + slot_rank, slot_total)
    token_of_pair = jnp.arange(pair_count, dtype=jnp.int32) // top_count
    spread = ffn_input[token_of_pair]
    packed = (
        jnp.zeros((slot_total, ffn_input.shape[1]), jnp.bfloat16)
        .at[buffer_slot]
        .set(spread, mode="drop")
    )
    arrived = lax.all_to_all(
        packed.reshape(dp_count, local_experts, capacity, ffn_input.shape[1]),
        "dp",
        split_axis=0,
        concat_axis=0,
        tiled=True,
    )
    gate_up = jnp.einsum(
        "secd,edkf->seckf", arrived, w_experts_in, preferred_element_type=jnp.float32
    )
    acting = (jax.nn.silu(gate_up[..., 0, :]) * gate_up[..., 1, :]).astype(jnp.bfloat16)
    expert_part = jnp.einsum(
        "secf,efd->secd", acting, w_experts_out, preferred_element_type=jnp.float32
    )
    expert_share = lax.psum_scatter(
        expert_part.astype(jnp.bfloat16), "head", scatter_dimension=3, tiled=True
    )
    returned = lax.all_to_all(expert_share, "dp", split_axis=0, concat_axis=0, tiled=True)
    returned_rows = returned.reshape(slot_total, share_width)
    pick_slot = jnp.minimum(buffer_slot, slot_total - 1)
    pair_rows = returned_rows[pick_slot].astype(jnp.float32)
    routed = jnp.sum(
        (route_weight.reshape(pair_count)[:, None] * pair_rows).reshape(
            request_count, top_count, share_width
        ),
        axis=1,
    )
    shared_width = w_shared_out.shape[0]
    shared_pair = jnp.dot(
        ffn_input,
        w_shared_in.reshape(model_width, 2 * shared_width),
        preferred_element_type=jnp.float32,
    ).reshape(request_count, 2, shared_width)
    shared_act = (jax.nn.silu(shared_pair[:, 0]) * shared_pair[:, 1]).astype(jnp.bfloat16)
    shared_part = jnp.dot(shared_act, w_shared_out, preferred_element_type=jnp.float32)
    shared_share = lax.psum_scatter(
        shared_part.astype(jnp.bfloat16), "head", scatter_dimension=1, tiled=True
    ).astype(jnp.float32)
    return (mixed_share.astype(jnp.float32) + shared_share + routed).astype(jnp.bfloat16)


def solution(mesh):
    placed = (
        P("dp", None),
        P(),
        P(None, "head"),
        P(None, "head"),
        P(),
        P("head", None, None),
        P("head", None, None),
        P("head", None),
        P("dp", None, None),
        P("dp"),
        P("dp"),
        P(),
        P(),
        P("dp", None),
        P("dp", None, None, "head"),
        P("dp", "head", None),
        P(None, None, "head"),
        P("head", None),
    )
    return jax.shard_map(
        body, mesh=mesh, in_specs=placed, out_specs=P("dp", "head"), check_vma=False
    )
```

profile of v0, /device:TPU:1, one launch (start us, length us, event | category | flops | bytes accessed | tf_op | source)
XLA Modules:
  0.0 187.7 jit_solution(8351223471823655975)
XLA Ops:
  6.6 0.8 convert_element_type.107
  7.4 0.9 iota_compare_fusion.2
  8.2 1.0 fusion.40
  9.3 1.5 fusion.29
  10.8 10.4 %all-gather = bf16[4,144,32]{1,2,0:T(8,128)(2,1)S(1)} all-gather(bf16[1,144,32]{1,2,0:T(8,128)(2,1)S(1)} %fusion.29), channel_id=1, replica_groups=mesh['dp'=32,'head'=4] {'head'}, dimensions={0}, use_global_device_ids=true | all-gather | bytes 46080 | tf_op jit(solution)/shard_map/all_gather | solution.py:81
  21.2 0.1 reshape.357
  21.3 0.1 fusion.50
  21.5 1.6 fusion.61
  23.0 0.1 reshape.311
  23.2 0.1 fusion.77
  23.3 0.1 fusion.75
  23.4 1.2 fusion.26
  24.7 0.1 subtract_convert_fusion.1
  24.8 0.1 maximum_bitcast_fusion
  24.9 0.1 pad_maximum_fusion
  25.0 0.3 fusion.46
  25.3 3.4 %fusion.78 = (f32[32,4]{1,0:T(8,128)S(1)}, f32[32,4,128]{2,1,0:T(4,128)S(1)}) fusion(bf16[32,128,576]{1,2,0:T(8,128)(2,1)} %param.26, bf16[32,4,576]{2,0,1:T(8,128)(2,1)S(1)} %pad_maximum_fusion, pred[32,128]{1,0:T(8,128)(4,1)S(1)} %iota_compare_fusion.2), kind=kOutput, calls=%fused_computation.128 | convolution fusion | flops 18923392 | bytes 4936192 | tf_op jit(solution)/shard_map/rhc,rjc->rhj/dot_general | solution.py:88
  28.7 0.2 fusion.57
  28.9 0.1 copy-done.1
  29.1 1.2 fusion.23
  30.3 0.2 fusion.28
  30.6 0.3 copy-done.3
  30.8 1.1 convolution_convert_fusion.1
  32.1 0.1 broadcast_in_dim.27
  32.1 0.1 eq.62
  32.2 0.1 eq.57
  32.4 0.1 copy.93
  32.5 0.1 copy.92
  32.6 0.1 mul.265
  32.7 0.1 eq.58
  32.8 0.6 reduce-window.6
  33.4 0.2 slice_reduce_fusion
  33.7 0.1 bitcast_bitcast_fusion
  33.8 41.9 %all-reduce.3.cloned.1.call-done = bf16[32,2048]{1,0:T(8,128)(2,1)} async-done(((bf16[32,2048]{1,0:T(8,128)(2,1)}), bf16[32,2048]{1,0:T(8,128)(2,1)}) %all-reduce.3.cloned.1.call-update) | async-done | bytes 131088 | tf_op jit(solution)/shard_map/psum | solution.py:116
  75.7 1.1 fusion.37
  76.8 0.6 copy-done.5
  77.4 0.1 fusion.39
  77.5 5.6 %scatter_custom_fusion = bf16[384,2048]{1,0:T(8,128)(2,1)} fusion(s32[192]{0:T(256)S(1)} %bitcast.114, bf16[32,2048]{1,0:T(8,128)(2,1)S(1)} %fusion.39, s32[1024]{0:T(1024)S(1)} %pad_clamp_fusion.1, bf16[]{:T(256)} %constant.75.clone.1), kind=kCustom, calls=%fused_computation.28 | custom fusion | bytes 1572866 | tf_op jit(solution)/shard_map/scatter | solution.py:144
  83.1 3.7 %reshape.317 = bf16[32,2,6,2048]{3,2,1,0:T(8,128)(2,1)} reshape(bf16[384,2048]{1,0:T(8,128)(2,1)} %scatter_custom_fusion) | data formatting | bytes 3145728 | tf_op jit(solution)/shard_map/reshape | solution.py:147
  86.8 3.2 %copy.96 = bf16[32,2,6,2048]{3,1,2,0:T(2,128)(2,1)S(1)} copy(bf16[32,2,6,2048]{3,2,1,0:T(8,128)(2,1)} %reshape.317) | data formatting | bytes 3145728 | tf_op jit(solution)/shard_map/reshape | solution.py:147
  90.0 32.3 %all_to_all.10 = bf16[32,2,6,2048]{3,1,2,0:T(2,128)(2,1)S(1)} all-to-all(bf16[32,2,6,2048]{3,1,2,0:T(2,128)(2,1)S(1)} %copy.96), channel_id=1, replica_groups=mesh['dp'=32,'head'=4] {'dp'}, dimensions={0} | all-to-all | bytes 3145728 | tf_op jit(solution)/shard_map/all_to_all | solution.py:146
  122.4 5.9 %fusion.15 = f32[32,2,6,2,352]{4,0,3,2,1:T(8,128)S(1)} fusion(bf16[2,2048,2,352]{1,3,2,0:T(8,128)(2,1)} %param.32, bf16[32,2,6,2048,1]{3,1,2,0,4:T(2,128)(2,1)S(1)} %bitcast.106), kind=kOutput, calls=%fused_computation.17 | convolution fusion | flops 1107296256 | bytes 8421376 | tf_op jit(solution)/shard_map/secd,edkf->seckf/dot_general | solution.py:153
  128.3 2.2 %fusion.11 = bf16[32,2,6,2048]{3,0,2,1:T(8,128)(2,1)} fusion(bf16[2,352,2048]{2,1,0:T(8,128)(2,1)S(1)} %copy-done.10, f32[32,2,6,2,352]{4,0,3,2,1:T(8,128)S(1)} %fusion.15), kind=kOutput, calls=%fused_computation.13 | convolution fusion | flops 555245568 | bytes 5537792 | tf_op jit(solution)/shard_map/secf,efd->secd/dot_general | solution.py:157
  130.5 0.1 copy.89
  130.6 0.1 reshape.337
  130.7 0.6 pad_clamp_fusion
  131.3 1.1 fusion.79
  132.4 1.6 gather_fusion.1
  134.1 0.1 reshape.340
  134.2 0.1 copy.90
  134.3 2.9 %fusion.6 = f32[32,2,352]{2,0,1:T(8,128)S(1)} fusion(bf16[2048,2,352]{0,2,1:T(8,128)(2,1)} %param.34, bf16[32,2048]{1,0:T(8,128)(2,1)S(1)} %fusion.39), kind=kOutput, calls=%fused_computation.10 | convolution fusion | flops 92274688 | bytes 3104768 | tf_op jit(solution)/shard_map/dot_general | solution.py:174
  137.2 1.0 convolution_convert_fusion
  138.3 13.7 %reduce-scatter.5.cloned.1.call-done = bf16[32,2,6,512]{3,0,2,1:T(8,128)(2,1)} async-done(((bf16[32,2,6,2048]{3,0,2,1:T(8,128)(2,1)}), bf16[32,2,6,512]{3,0,2,1:T(8,128)(2,1)}) %reduce-scatter.5.cloned.1.call-update) | async-done | bytes 393232 | tf_op jit(solution)/shard_map/reduce_scatter | solution.py:160
  151.9 2.1 %copy.99 = bf16[32,2,6,512]{3,1,2,0:T(2,128)(2,1)} copy(bf16[32,2,6,512]{3,0,2,1:T(8,128)(2,1)} %reduce-scatter.5.cloned.1.call-done) | data formatting | bytes 786432 | tf_op jit(solution)/shard_map/reduce_scatter | solution.py:160
  154.1 8.6 %all-to-all-start.1 = ((bf16[32,2,6,512]{3,1,2,0:T(2,128)(2,1)}), bf16[32,2,6,512]{3,1,2,0:T(2,128)(2,1)S(1)}, u32[]{:S(2)}, u32[]{:S(2)}) async-start(bf16[32,2,6,512]{3,1,2,0:T(2,128)(2,1)} %copy.99), calls=%async_computation.3 | async-start | bytes 786432 | tf_op jit(solution)/shard_map/all_to_all | solution.py:163
  162.7 0.6 multiply_divide_fusion
  163.3 0.8 copy.91
  164.0 8.8 %all-to-all-done.1 = bf16[32,2,6,512]{3,1,2,0:T(2,128)(2,1)S(1)} async-done(((bf16[32,2,6,512]{3,1,2,0:T(2,128)(2,1)}), bf16[32,2,6,512]{3,1,2,0:T(2,128)(2,1)S(1)}, u32[]{:S(2)}, u32[]{:S(2)}) %all-to-all-start.1) | async-done | bytes 393248 | tf_op jit(solution)/shard_map/all_to_all | solution.py:163
  172.8 0.9 copy.100
  173.7 1.2 reshape.318
  174.9 1.8 gather_fusion
  176.7 1.8 reshape.320
  178.4 1.3 multiply_reduce_fusion
  179.7 1.4 add_convert_fusion
  (51 shorter events, 0.6 us)
Async XLA Ops:
  6.5 14.9 %copy-start = (bf16[2048,768]{1,0:T(8,128)(2,1)S(1)}, bf16[2048,768]{1,0:T(8,128)(2,1)}, u32[]{:S(2)}) copy-start(bf16[2048,768]{1,0:T(8,128)(2,1)} %param.20) | copy-start | bytes 9437188
  6.5 69.2 %all-reduce.3.cloned.1.call-start = ((), (), s32[]{:S(2)}) async-start(), calls=%async_computation.4 | async-start | bytes 262144 | tf_op jit(solution)/shard_map/psum | solution.py:116
  21.2 2.2 %copy-start.9 = (f32[512]{0:T(512)S(1)}, f32[512]{0:T(512)}, u32[]{:S(2)}) copy-start(f32[512]{0:T(512)} %param.22) | copy-start | bytes 6148
  25.3 3.8 %copy-start.1 = (bf16[32,128,576]{1,2,0:T(8,128)(2,1)S(1)}, bf16[32,128,576]{1,2,0:T(8,128)(2,1)}, u32[]{:S(2)}) copy-start(bf16[32,128,576]{1,2,0:T(8,128)(2,1)} %param.26) | copy-start | bytes 14155780
  29.1 1.2 copy-start.6
  29.1 1.8 copy-start.3
  30.3 1.7 copy-start.11
  30.3 2.1 %copy-start.7 = (s32[32,6]{0,1:T(8,128)S(1)}, s32[32,6]{0,1:T(8,128)}, u32[]{:S(2)}) copy-start(s32[32,6]{0,1:T(8,128)} %param.31) | copy-start | bytes 2308
  30.3 45.4 %copy-start.2 = (bf16[32,2048]{1,0:T(8,128)(2,1)S(1)}, bf16[32,2048]{1,0:T(8,128)(2,1)}, u32[]{:S(2)}) copy-start(bf16[32,2048]{1,0:T(8,128)(2,1)} %param.18) | copy-start | bytes 393220
  30.3 47.1 %copy-start.8 = (f32[2048]{0:T(1024)S(1)}, f32[2048]{0:T(1024)}, u32[]{:S(2)}) copy-start(f32[2048]{0:T(1024)} %param.29) | copy-start | bytes 24580
  32.0 120.0 %reduce-scatter.5.cloned.1.call-start = ((), (), s32[]{:S(2)}) async-start(), calls=%async_computation.6 | async-start | bytes 1966080 | tf_op jit(solution)/shard_map/reduce_scatter | solution.py:160
  76.8 0.6 copy-start.5
  122.4 5.9 %copy-start.10 = (bf16[2,352,2048]{2,1,0:T(8,128)(2,1)S(1)}, bf16[2,352,2048]{2,1,0:T(8,128)(2,1)}, u32[]{:S(2)}) copy-start(bf16[2,352,2048]{2,1,0:T(8,128)(2,1)} %param.33) | copy-start | bytes 8650756
  130.4 49.3 %reduce-scatter.3.cloned.1.call-start = ((), (), s32[]{:S(2)}) async-start(), calls=%async_computation.5 | async-start | bytes 163840 | tf_op jit(solution)/shard_map/reduce_scatter | solution.py:181
  134.3 3.0 %copy-start.4 = (bf16[352,2048]{1,0:T(8,128)(2,1)S(1)}, bf16[352,2048]{1,0:T(8,128)(2,1)}, u32[]{:S(2)}) copy-start(bf16[352,2048]{1,0:T(8,128)(2,1)} %param.35) | copy-start | bytes 4325380
  154.1 18.7 %all-to-all-start.1 = ((bf16[32,2,6,512]{3,1,2,0:T(2,128)(2,1)}), bf16[32,2,6,512]{3,1,2,0:T(2,128)(2,1)S(1)}, u32[]{:S(2)}, u32[]{:S(2)}) async-start(bf16[32,2,6,512]{3,1,2,0:T(2,128)(2,1)} %copy.99), calls=%async_computation.3 | async-start | bytes 786432 | tf_op jit(solution)/shard_map/all_to_all | solution.py:163
Sparse Core Ops, SparseCore 0:
  32.1 43.5 all-reduce.2
  130.6 21.3 reduce-scatter.4
  154.4 19.3 reduce-scatter.2
where the time goes:
time: 188 us
  waiting for transfers between devices  64.4 us (34%)
  blocking collectives  42.7 us (23%)
  local copies, waits for them, and re-layouts  25.4 us (14%)
  matrix products  23.6 us (13%)
  between operations  13.4 us (7%)
  other arithmetic  9.43 us (5%)
  starting transfers between devices  8.64 us (5%)
    psum x1, waiting for transfers between devices, body(): lax.psum(partial_value.astype(jnp.bfloat16), 'head').astype(jnp.float32)  41.9 us
    all_to_all x1, blocking collectives, body(): lax.all_to_all(packed.reshape(dp_count, local_experts, capacity, ffn_inpu...  32.3 us
    reduce_scatter x1, waiting for transfers between devices, body(): lax.psum_scatter(expert_part.astype(jnp.bfloat16), 'head', scatter_dimens...  13.7 us
    all_gather x1, blocking collectives, body(): fresh_kv = lax.all_gather(fresh_part, 'head', axis=1, tiled=True)  10.4 us
    all_to_all x1, waiting for transfers between devices, body(): lax.all_to_all(expert_share, 'dp', split_axis=0, concat_axis=0, tiled=True)  8.77 us
    all_to_all x1, starting transfers between devices, body(): lax.all_to_all(expert_share, 'dp', split_axis=0, concat_axis=0, tiled=True)  8.56 us
    reshape x2, local copies, waits for them, and re-layouts, body(): packed.reshape(dp_count, local_experts, capacity, ffn_input.shape[1])  6.93 us
    dot_general x1, matrix products, body(): jnp.einsum('secd,edkf->seckf', arrived, w_experts_in, preferred_element_t...  5.86 us
  transfers between devices with their start and end apart: 4, of which 3 were waited for; matrix products, arithmetic and copies ran while one was open for 11% of the time, Pallas kernels for 0%

commit v1 on v0

--- a/solution.py
+++ b/solution.py
@@ -78,7 +78,16 @@
         "rhn,hnc->rhc", query_nope, w_key_up, preferred_element_type=jnp.float32
     ).astype(jnp.bfloat16)
     fresh_part = jnp.dot(normed, w_latent, preferred_element_type=jnp.float32).astype(jnp.bfloat16)
-    fresh_kv = lax.all_gather(fresh_part, "head", axis=1, tiled=True)
+    ways = lax.axis_size("head")
+    up = [(d, (d + 1) % ways) for d in range(ways)]
+    down = [(d, (d - 1) % ways) for d in range(ways)]
+    earlier_2, later = ([fresh_part], [fresh_part])
+    for _ in range(ways // 2):
+        earlier_2.append(lax.ppermute(earlier_2[-1], "head", up))
+    for _ in range((ways - 1) // 2):
+        later.append(lax.ppermute(later[-1], "head", down))
+    line = jnp.concatenate([*earlier_2[::-1], *later[1:]], axis=1)
+    fresh_kv = jnp.roll(line, (lax.axis_index("head") - ways // 2) * fresh_part.shape[1], axis=1)
     latent_new = rms_norm(fresh_kv[:, :LAT].astype(jnp.float32), latent_gain)
     rope_new = rotary(fresh_kv[:, LAT:].astype(jnp.float32), positions)
     key_new = jnp.concatenate([latent_new, rope_new], axis=-1).astype(jnp.bfloat16)

time: 188 us -> 191 us (1.016)
  blocking collectives: 42.7 us -> 32.3 us
  other arithmetic: 9.43 us -> 13.7 us
  starting transfers between devices: 8.64 us -> 12.3 us
  local copies, waits for them, and re-layouts: 25.4 us -> 28.8 us
    all_gather x1 -> x0, blocking collectives: 10.4 us -> none  [body(): fresh_kv = lax.all_gather(fresh_part, 'head', axis=1, tiled=True)]
    ppermute x0 -> x3, starting transfers between devices: none -> 3.66 us  [the longest x1 3.63 us: body(): later.append(lax.ppermute(later[-1], 'head', down))]
  transfers between devices with their start and end apart: 4 -> 7, of which waited for: 3 -> 4; matrix products, arithmetic and copies ran while one was open for 11% -> 16% of each run, Pallas kernels for 0% -> 0%
where the time goes in v1:
time: 191 us; the launch traced here: 190 us
  waiting for transfers between devices  65.8 us (34%)
  blocking collectives  32.3 us (17%)
  local copies, waits for them, and re-layouts  28.8 us (15%)
  matrix products  23.6 us (12%)
  other arithmetic  13.7 us (7%)
  between operations  13.5 us (7%)
  starting transfers between devices  12.3 us (6%)
    psum x1, waiting for transfers between devices, body(): lax.psum(partial_value.astype(jnp.bfloat16), 'head').astype(jnp.float32)  41.9 us
    all_to_all x1, blocking collectives, body(): lax.all_to_all(packed.reshape(dp_count, local_experts, capacity, ffn_inpu...  32.3 us
    reduce_scatter x1, waiting for transfers between devices, body(): lax.psum_scatter(expert_part.astype(jnp.bfloat16), 'head', scatter_dimens...  13.6 us
    all_to_all x1, waiting for transfers between devices, body(): lax.all_to_all(expert_share, 'dp', split_axis=0, concat_axis=0, tiled=True)  8.77 us
    all_to_all x1, starting transfers between devices, body(): lax.all_to_all(expert_share, 'dp', split_axis=0, concat_axis=0, tiled=True)  8.56 us
    reshape x2, local copies, waits for them, and re-layouts, body(): packed.reshape(dp_count, local_experts, capacity, ffn_input.shape[1])  6.93 us
    dot_general x1, matrix products, body(): jnp.einsum('secd,edkf->seckf', arrived, w_experts_in, preferred_element_t...  5.86 us
    scatter x1, local copies, waits for them, and re-layouts, body(): packed = jnp.zeros((slot_total, ffn_input.shape[1]), jnp.bfloat16).at[buf...  5.57 us
  transfers between devices with their start and end apart: 7, of which 4 were waited for; matrix products, arithmetic and copies ran while one was open for 16% of the time, Pallas kernels for 0%

profile of v1, /device:TPU:1, one launch (start us, length us, event | category | flops | bytes accessed | tf_op | source)
XLA Modules:
  0.0 189.9 jit_solution(6499087345340638330)
XLA Ops:
  6.5 1.2 fusion.39
  7.7 1.5 convolution_convert_fusion.4
  9.2 3.6 %collective-permute-start.2 = (bf16[32,144]{1,0:T(8,128)(2,1)S(1)}, bf16[32,144]{1,0:T(8,128)(2,1)S(1)}, u32[]{:S(2)}, u32[]{:S(2)}) collective-permute-start(bf16[32,144]{1,0:T(8,128)(2,1)S(1)} %convolution_convert_fusion.4), channel_id=1, source_target_pairs={{0,3},{1,0},{2,1},{3,2},{4,7},{5,4},{6,5},{7,6},{8,11},{9,8},{10,9... | collective-permute-start | bytes 27656 | tf_op jit(solution)/shard_map/ppermute | solution.py:88
  12.9 0.7 broadcast_multiply_fusion
  13.6 1.4 copy.89
  14.9 1.6 fusion.60
  16.5 0.1 reshape.311
  16.7 0.1 fusion.76
  16.9 0.1 eq.65
  17.0 0.7 iota_compare_fusion.2
  17.8 0.8 eq.61
  18.6 0.6 reduce-window.6
  19.2 0.2 slice_reduce_fusion
  19.5 0.1 bitcast_bitcast_fusion
  19.6 1.2 fusion.26
  20.8 1.2 fusion.53
  22.0 0.5 multiply_power_fusion
  22.6 1.2 convert_element_type.107
  23.7 0.7 eq.60
  24.5 0.1 mul.269
  24.6 1.4 collective-permute-done.1
  26.0 0.9 concatenate.17
  26.9 0.2 fusion.49
  27.1 0.1 dynamic-slice_convert_fusion
  27.2 0.8 fusion.74
  28.0 0.8 subtract_convert_fusion.1
  29.0 0.3 fusion.45
  29.3 3.4 %fusion.77 = (f32[32,4]{1,0:T(8,128)S(1)}, f32[32,4,128]{2,1,0:T(4,128)S(1)}) fusion(bf16[32,128,576]{1,2,0:T(8,128)(2,1)} %param.26, bf16[32,4,576]{2,0,1:T(8,128)(2,1)S(1)} %pad_maximum_fusion, pred[32,128]{1,0:T(8,128)(4,1)S(1)} %iota_compare_fusion.2), kind=kOutput, calls=%fused_computation.127 | convolution fusion | flops 18923392 | bytes 4936192 | tf_op jit(solution)/shard_map/rhc,rjc->rhj/dot_general | solution.py:97
  32.7 0.2 fusion.56
  32.9 0.1 copy-done.1
  33.0 1.2 fusion.23
  34.3 0.2 fusion.28
  34.5 0.3 copy-done.3
  34.8 1.1 convolution_convert_fusion.1
  36.1 41.9 %all-reduce.3.cloned.1.call-done = bf16[32,2048]{1,0:T(8,128)(2,1)} async-done(((bf16[32,2048]{1,0:T(8,128)(2,1)}), bf16[32,2048]{1,0:T(8,128)(2,1)}) %all-reduce.3.cloned.1.call-update) | async-done | bytes 131088 | tf_op jit(solution)/shard_map/psum | solution.py:125
  78.0 1.1 fusion.36
  79.0 0.6 copy-done.5
  79.7 0.1 fusion.38
  79.8 5.6 %scatter_custom_fusion = bf16[384,2048]{1,0:T(8,128)(2,1)} fusion(s32[192]{0:T(256)S(1)} %bitcast.105, bf16[32,2048]{1,0:T(8,128)(2,1)S(1)} %fusion.38, s32[1024]{0:T(1024)S(1)} %pad_clamp_fusion.1, bf16[]{:T(256)} %constant.98.clone.1), kind=kCustom, calls=%fused_computation.27 | custom fusion | bytes 1572866 | tf_op jit(solution)/shard_map/scatter | solution.py:153
  85.3 3.7 %reshape.317 = bf16[32,2,6,2048]{3,2,1,0:T(8,128)(2,1)} reshape(bf16[384,2048]{1,0:T(8,128)(2,1)} %scatter_custom_fusion) | data formatting | bytes 3145728 | tf_op jit(solution)/shard_map/reshape | solution.py:156
  89.0 3.2 %copy.92 = bf16[32,2,6,2048]{3,1,2,0:T(2,128)(2,1)S(1)} copy(bf16[32,2,6,2048]{3,2,1,0:T(8,128)(2,1)} %reshape.317) | data formatting | bytes 3145728 | tf_op jit(solution)/shard_map/reshape | solution.py:156
  92.3 32.3 %all_to_all.10 = bf16[32,2,6,2048]{3,1,2,0:T(2,128)(2,1)S(1)} all-to-all(bf16[32,2,6,2048]{3,1,2,0:T(2,128)(2,1)S(1)} %copy.92), channel_id=1, replica_groups=mesh['dp'=32,'head'=4] {'dp'}, dimensions={0} | all-to-all | bytes 3145728 | tf_op jit(solution)/shard_map/all_to_all | solution.py:155
  124.6 5.9 %fusion.15 = f32[32,2,6,2,352]{4,0,3,2,1:T(8,128)S(1)} fusion(bf16[2,2048,2,352]{1,3,2,0:T(8,128)(2,1)} %param.32, bf16[32,2,6,2048,1]{3,1,2,0,4:T(2,128)(2,1)S(1)} %bitcast.99), kind=kOutput, calls=%fused_computation.17 | convolution fusion | flops 1107296256 | bytes 8421376 | tf_op jit(solution)/shard_map/secd,edkf->seckf/dot_general | solution.py:162
  130.5 2.2 %fusion.11 = bf16[32,2,6,2048]{3,0,2,1:T(8,128)(2,1)} fusion(bf16[2,352,2048]{2,1,0:T(8,128)(2,1)S(1)} %copy-done.12, f32[32,2,6,2,352]{4,0,3,2,1:T(8,128)S(1)} %fusion.15), kind=kOutput, calls=%fused_computation.13 | convolution fusion | flops 555245568 | bytes 5537792 | tf_op jit(solution)/shard_map/secf,efd->secd/dot_general | solution.py:166
  132.8 0.1 copy.85
  132.9 0.1 reshape.337
  133.0 0.6 pad_clamp_fusion
  133.6 1.1 fusion.78
  134.7 1.6 gather_fusion.1
  136.3 0.1 reshape.340
  136.5 2.9 %fusion.6 = f32[32,2,352]{2,0,1:T(8,128)S(1)} fusion(bf16[2048,2,352]{0,2,1:T(8,128)(2,1)} %param.34, bf16[32,2048]{1,0:T(8,128)(2,1)S(1)} %fusion.38), kind=kOutput, calls=%fused_computation.10 | convolution fusion | flops 92274688 | bytes 3104768 | tf_op jit(solution)/shard_map/dot_general | solution.py:183
  139.5 1.0 convolution_convert_fusion
  140.5 13.6 %reduce-scatter.5.cloned.1.call-done = bf16[32,2,6,512]{3,0,2,1:T(8,128)(2,1)} async-done(((bf16[32,2,6,2048]{3,0,2,1:T(8,128)(2,1)}), bf16[32,2,6,512]{3,0,2,1:T(8,128)(2,1)}) %reduce-scatter.5.cloned.1.call-update) | async-done | bytes 393232 | tf_op jit(solution)/shard_map/reduce_scatter | solution.py:169
  154.2 2.1 %copy.95 = bf16[32,2,6,512]{3,1,2,0:T(2,128)(2,1)} copy(bf16[32,2,6,512]{3,0,2,1:T(8,128)(2,1)} %reduce-scatter.5.cloned.1.call-done) | data formatting | bytes 786432 | tf_op jit(solution)/shard_map/reduce_scatter | solution.py:169
  156.3 8.6 %all-to-all-start.1 = ((bf16[32,2,6,512]{3,1,2,0:T(2,128)(2,1)}), bf16[32,2,6,512]{3,1,2,0:T(2,128)(2,1)S(1)}, u32[]{:S(2)}, u32[]{:S(2)}) async-start(bf16[32,2,6,512]{3,1,2,0:T(2,128)(2,1)} %copy.95), calls=%async_computation.3 | async-start | bytes 786432 | tf_op jit(solution)/shard_map/all_to_all | solution.py:172
  164.9 0.6 multiply_divide_fusion
  165.5 0.8 copy.87
  166.3 8.8 %all-to-all-done.1 = bf16[32,2,6,512]{3,1,2,0:T(2,128)(2,1)S(1)} async-done(((bf16[32,2,6,512]{3,1,2,0:T(2,128)(2,1)}), bf16[32,2,6,512]{3,1,2,0:T(2,128)(2,1)S(1)}, u32[]{:S(2)}, u32[]{:S(2)}) %all-to-all-start.1) | async-done | bytes 393248 | tf_op jit(solution)/shard_map/all_to_all | solution.py:172
  175.1 0.9 copy.96
  175.9 1.2 reshape.318
  177.1 1.8 gather_fusion
  178.9 1.8 reshape.320
  180.7 1.3 multiply_reduce_fusion
  182.0 1.4 add_convert_fusion
  (60 shorter events, 0.9 us)
Async XLA Ops:
  6.5 8.4 %copy-start = (bf16[2048,768]{1,0:T(8,128)(2,1)S(1)}, bf16[2048,768]{1,0:T(8,128)(2,1)}, u32[]{:S(2)}) copy-start(bf16[2048,768]{1,0:T(8,128)(2,1)} %param.20) | copy-start | bytes 9437188
  6.5 71.4 %all-reduce.3.cloned.1.call-start = ((), (), s32[]{:S(2)}) async-start(), calls=%async_computation.4 | async-start | bytes 262144 | tf_op jit(solution)/shard_map/psum | solution.py:125
  9.2 7.6 %copy-start.13 = (s32[32]{0:T(128)S(1)}, s32[32]{0:T(128)}, u32[]{:S(2)}) copy-start(s32[32]{0:T(128)} %param.28) | copy-start | bytes 388
  9.2 15.4 %collective-permute-start.2 = (bf16[32,144]{1,0:T(8,128)(2,1)S(1)}, bf16[32,144]{1,0:T(8,128)(2,1)S(1)}, u32[]{:S(2)}, u32[]{:S(2)}) collective-permute-start(bf16[32,144]{1,0:T(8,128)(2,1)S(1)} %convolution_convert_fusion.4), channel_id=1, source_target_pairs={{0,3},{1,0},{2,1},{3,2},{4,7},{5,4},{6,5},{7,6},{8,11},{9,8},{10,9... | collective-permute-start | bytes 27656 | tf_op jit(solution)/shard_map/ppermute | solution.py:88
  12.9 9.1 %collective-permute-start = (bf16[32,144]{1,0:T(8,128)(2,1)S(1)}, bf16[32,144]{1,0:T(8,128)(2,1)}, u32[]{:S(2)}, u32[]{:S(2)}) collective-permute-start(bf16[32,144]{1,0:T(8,128)(2,1)S(1)} %convolution_convert_fusion.4), channel_id=1, source_target_pairs={{0,1},{1,2},{2,3},{3,0},{4,5},{5,6},{6,7},{7,4},{8,9},{9,10},{10,1... | collective-permute-start | bytes 27656 | tf_op jit(solution)/shard_map/ppermute | solution.py:86
  17.0 2.4 %copy-start.9 = (pred[192]{0:T(512)(128)(4,1)}, pred[192]{0:T(512)(128)(4,1)S(1)}, u32[]{:S(2)}) copy-start(pred[192]{0:T(512)(128)(4,1)S(1)} %eq.65) | copy-start | bytes 580
  22.0 4.0 %collective-permute-start.1 = (bf16[32,144]{1,0:T(8,128)(2,1)}, bf16[32,144]{1,0:T(8,128)(2,1)S(1)}, u32[]{:S(2)}, u32[]{:S(2)}) collective-permute-start(bf16[32,144]{1,0:T(8,128)(2,1)} %collective-permute-done), channel_id=1, source_target_pairs={{0,1},{1,2},{2,3},{3,0},{4,5},{5,6},{6,7},{7,4},{8,9},{9,10},{10,1... | collective-permute-start | bytes 27656 | tf_op jit(solution)/shard_map/ppermute | solution.py:86
  29.3 3.8 %copy-start.1 = (bf16[32,128,576]{1,2,0:T(8,128)(2,1)S(1)}, bf16[32,128,576]{1,2,0:T(8,128)(2,1)}, u32[]{:S(2)}) copy-start(bf16[32,128,576]{1,2,0:T(8,128)(2,1)} %param.26) | copy-start | bytes 14155780
  33.0 1.2 copy-start.6
  33.0 1.8 copy-start.3
  34.3 1.7 copy-start.10
  34.3 1.7 copy-start.11
  34.3 43.7 %copy-start.2 = (bf16[32,2048]{1,0:T(8,128)(2,1)S(1)}, bf16[32,2048]{1,0:T(8,128)(2,1)}, u32[]{:S(2)}) copy-start(bf16[32,2048]{1,0:T(8,128)(2,1)} %param.18) | copy-start | bytes 393220
  34.3 45.3 %copy-start.8 = (f32[2048]{0:T(1024)S(1)}, f32[2048]{0:T(1024)}, u32[]{:S(2)}) copy-start(f32[2048]{0:T(1024)} %param.29) | copy-start | bytes 24580
  36.0 118.2 %reduce-scatter.5.cloned.1.call-start = ((), (), s32[]{:S(2)}) async-start(), calls=%async_computation.6 | async-start | bytes 1966080 | tf_op jit(solution)/shard_map/reduce_scatter | solution.py:169
  79.0 0.6 copy-start.5
  124.6 5.9 %copy-start.12 = (bf16[2,352,2048]{2,1,0:T(8,128)(2,1)S(1)}, bf16[2,352,2048]{2,1,0:T(8,128)(2,1)}, u32[]{:S(2)}) copy-start(bf16[2,352,2048]{2,1,0:T(8,128)(2,1)} %param.33) | copy-start | bytes 8650756
  130.5 2.3 %copy-start.7 = (s32[32,6]{0,1:T(8,128)S(1)}, s32[32,6]{0,1:T(8,128)}, u32[]{:S(2)}) copy-start(s32[32,6]{0,1:T(8,128)} %param.31) | copy-start | bytes 2308
  130.5 3.1 %copy-start.14 = (s32[32]{0:T(128)S(1)}, s32[32]{0:T(128)}, u32[]{:S(2)}) copy-start(s32[32]{0:T(128)} %param.28) | copy-start | bytes 388
  132.7 49.3 %reduce-scatter.3.cloned.1.call-start = ((), (), s32[]{:S(2)}) async-start(), calls=%async_computation.5 | async-start | bytes 163840 | tf_op jit(solution)/shard_map/reduce_scatter | solution.py:190
  136.5 3.0 %copy-start.4 = (bf16[352,2048]{1,0:T(8,128)(2,1)S(1)}, bf16[352,2048]{1,0:T(8,128)(2,1)}, u32[]{:S(2)}) copy-start(bf16[352,2048]{1,0:T(8,128)(2,1)} %param.35) | copy-start | bytes 4325380
  156.3 18.7 %all-to-all-start.1 = ((bf16[32,2,6,512]{3,1,2,0:T(2,128)(2,1)}), bf16[32,2,6,512]{3,1,2,0:T(2,128)(2,1)S(1)}, u32[]{:S(2)}, u32[]{:S(2)}) async-start(bf16[32,2,6,512]{3,1,2,0:T(2,128)(2,1)} %copy.95), calls=%async_computation.3 | async-start | bytes 786432 | tf_op jit(solution)/shard_map/all_to_all | solution.py:172
Sparse Core Ops, SparseCore 0:
  36.1 41.8 all-reduce.2
  132.8 21.3 reduce-scatter.4
  156.7 19.3 reduce-scatter.2
